TPU v7x, 256 devices: a whole 4x4x8 slice. The times are simulated.
256 devices in a mesh: atoms: 32 (over z, x), bands: 8 (over y, core).
Axes of the slice: x: 4, y: 4, z: 8, core: 2. Of those that a mesh axis runs over, the one named last changes fastest.
Arguments:
- eigvecs: bfloat16 [32768, 8192], P('atoms', 'bands'), may hold values from -0.59765625 to 0.59765625
- occupations: float32 [8192], P('bands'), may hold values from 0.2 to 2
- energies: float32 [8192], P('bands'), may hold values from -1 to 0.5
- neighbours: int32 [256, 16], P('atoms'), may hold values from 0 to 255, as said below
Outputs:
- density: float32 [256, 16, 128, 128], P('atoms', None, 'bands')
- energy_density: float32 [256, 16, 128, 128], P('atoms', None, 'bands')
Inputs may be any that keep to these rules, and one draw needn't show every extreme that they name: `neighbours`: every block named in the rows of one atoms domain lies in that domain or in one of the 2 domains on either side along the atoms axis, taken cyclically; from each of those 4 other domains the rows of one domain name exactly 2 distinct blocks.
All inputs are finite; a program needn't handle non-finite values.
Results may differ from a plain program's by a relative error of at most 0.014.
Values may be sent and summed in bfloat16 or wider, within the bound.
A program may use at most 128 MiB of HBM per device.

v0:
```python
import jax
import jax.numpy as jnp
from jax import lax
from jax.sharding import PartitionSpec as P

CAP = 2
R = 2


def shifted(value, axis, steps):
    count = lax.axis_size(axis)
    pairs = [(source, (source + steps) % count) for source in range(count)]
    return lax.ppermute(value, axis, pairs)


def body(eigvecs, occupations, energies, neighbours):
    n_atoms = lax.axis_size("atoms")
    own_index = lax.axis_index("atoms")
    blocks_dev, neigh_count = neighbours.shape
    tile_rows = eigvecs.shape[0] // blocks_dev
    band_dev = eigvecs.shape[1]
    total_blocks = blocks_dev * n_atoms
    local_rows = eigvecs.reshape(blocks_dev, tile_rows, band_dev)
    flat_ids = neighbours.reshape(-1)
    owners = flat_ids // blocks_dev
    within = flat_ids % blocks_dev
    distance = (owners - own_index) % n_atoms
    slot_group = jnp.where(distance <= R, distance + R - 1, distance - n_atoms + R)
    offsets = list(range(-R, 0)) + list(range(1, R + 1))
    hits = flat_ids[:, None] == jnp.arange(total_blocks, dtype=jnp.int32)[None, :]
    needed = jnp.any(hits, axis=0).reshape(n_atoms, blocks_dev)
    needed = needed & (jnp.arange(n_atoms, dtype=jnp.int32)[:, None] != own_index)
    needed_int = needed.astype(jnp.int32)
    ranks = jnp.cumsum(needed_int, axis=1) - needed_int
    select = needed[:, :, None] & (
        ranks[:, :, None] == jnp.arange(CAP, dtype=jnp.int32)[None, None, :]
    )
    block_numbers = jnp.arange(blocks_dev, dtype=jnp.int32)[None, :, None]
    wanted = jnp.sum(select.astype(jnp.int32) * block_numbers, axis=1)

    def deliver(offset):
        target = (own_index + offset) % n_atoms
        request = lax.dynamic_index_in_dim(wanted, target, 0, keepdims=False)
        asked = shifted(request, "atoms", offset)
        return shifted(local_rows[asked], "atoms", -offset)

    arrived = jnp.concatenate([deliver(offset) for offset in offsets], 0)
    flat_ranks = ranks.reshape(-1)[flat_ids]
    remote_place = blocks_dev + slot_group * CAP + flat_ranks
    position = jnp.where(owners == own_index, within, remote_place)
    positions = position.reshape(blocks_dev, neigh_count)
    available = jnp.concatenate([local_rows, arrived], 0)
    weight_energy = occupations * energies
    scaled = jnp.stack([local_rows * occupations, local_rows * weight_energy], 1).astype(
        jnp.bfloat16
    )

    def one_block(pair):
        left, where_rows = pair
        right = available[where_rows]
        return jnp.einsum("sab,kcb->ksac", left, right, preferred_element_type=jnp.float32)

    partial_value = lax.map(one_block, (scaled, positions))
    summed = lax.psum_scatter(
        partial_value.astype(jnp.bfloat16), "bands", scatter_dimension=3, tiled=True
    ).astype(jnp.float32)
    return (summed[:, :, 0], summed[:, :, 1])


def solution(mesh):
    return jax.shard_map(
        body,
        mesh=mesh,
        in_specs=(P("atoms", "bands"), P("bands"), P("bands"), P("atoms", None)),
        out_specs=(P("atoms", None, "bands", None), P("atoms", None, "bands", None)),
        check_vma=False,
    )
```

profile of v0, /device:TPU:8, one launch (start us, length us, event | category | flops | bytes accessed | tf_op | source)
XLA Modules:
  0.0 222.6 jit_solution(9436073162178896825)
XLA Ops:
  8.9 8.4 %collective-permute-start = (s32[2]{0:T(128)S(1)}, s32[2]{0:T(128)S(1)}, u32[]{:S(2)}, u32[]{:S(2)}) collective-permute-start(s32[2]{0:T(128)S(1)} %get-tuple-element.33), channel_id=1, source_target_pairs={{0,240},{8,248},{16,0},{24,8},{32,16},{40,24},{48,32},{56,40},{64,... | collective-permute-start | bytes 32 | tf_op jit(solution)/shard_map/ppermute | solution.py:13
  23.8 2.5 %fusion.10 = (bf16[8,1,128,1024]{3,2,1,0:T(8,128)(2,1)S(1)}, bf16[8,1,128,1024]{3,2,1,0:T(8,128)(2,1)S(1)}) fusion(bf16[8,1,128,1024]{3,2,1,0:T(8,128)(2,1)} %bitcast.42, f32[1024]{0:T(1024)} %param.7, f32[1024]{0:T(1024)S(1)} %mul.50), kind=kLoop, calls=%fused_computation.20 | loop fusion | flops 5242880 | bytes 6299648 | tf_op jit(solution)/shard_map/convert.1
  33.0 5.3 %collective-permute-start.5 = (bf16[2,128,1024]{2,1,0:T(8,128)(2,1)}, bf16[2,128,1024]{2,1,0:T(8,128)(2,1)}, u32[]{:S(2)}, u32[]{:S(2)}) collective-permute-start(bf16[2,128,1024]{2,1,0:T(8,128)(2,1)} %gather_fusion.4), channel_id=1, source_target_pairs={{0,248},{8,0},{16,8},{24,16},{32,24},{40,32},{48,40},{56,48},{64,5... | collective-permute-start | bytes 1572872 | tf_op jit(solution)/shard_map/ppermute | solution.py:13
  42.2 6.5 %collective-permute-done.1 = bf16[2,128,1024]{2,1,0:T(8,128)(2,1)S(1)} collective-permute-done((bf16[2,128,1024]{2,1,0:T(8,128)(2,1)}, bf16[2,128,1024]{2,1,0:T(8,128)(2,1)S(1)}, u32[]{:S(2)}, u32[]{:S(2)}) %collective-permute-start.1) | collective-permute-done | bytes 524320 | tf_op jit(solution)/shard_map/ppermute | solution.py:13
  48.7 10.8 %collective-permute-done.3 = bf16[2,128,1024]{2,1,0:T(8,128)(2,1)S(1)} collective-permute-done((bf16[2,128,1024]{2,1,0:T(8,128)(2,1)}, bf16[2,128,1024]{2,1,0:T(8,128)(2,1)S(1)}, u32[]{:S(2)}, u32[]{:S(2)}) %collective-permute-start.3) | collective-permute-done | bytes 524320 | tf_op jit(solution)/shard_map/ppermute | solution.py:13
  59.5 15.6 %collective-permute-done.5 = bf16[2,128,1024]{2,1,0:T(8,128)(2,1)} collective-permute-done((bf16[2,128,1024]{2,1,0:T(8,128)(2,1)}, bf16[2,128,1024]{2,1,0:T(8,128)(2,1)}, u32[]{:S(2)}, u32[]{:S(2)}) %collective-permute-start.5) | collective-permute-done | bytes 524320 | tf_op jit(solution)/shard_map/ppermute | solution.py:13
  78.2 83.0 %while.10 = (s32[]{:T(128)}, bf16[8,16,2,128,128]{4,3,1,0,2:T(8,128)(2,1)}, s32[8,16]{1,0:T(8,128)S(1)}, bf16[16,128,1024]{2,1,0:T(8,128)(2,1)}, bf16[8,2,128,1024]{3,2,1,0:T(8,128)(2,1)}, /*index=5*/s32[]{:T(128)}) while((s32[]{:T(128)}, bf16[8,16,2,128,128]{4,3,1,0,2:T(8,128)(2,1)}, s32[8,16]{1,0:T(8,128)S(1)}, ...), condition=%wide.region_4.5_spmd, body=%wide.region_3.4_spmd.sunk | while | flops 1073742848 | bytes 18355528 | solution.py:63
  78.2 4.9 %gather_fusion = bf16[16,128,1024]{2,1,0:T(8,128)(2,1)} fusion(bf16[16,128,1024]{2,1,0:T(8,128)(2,1)} %get-tuple-element.100, s32[1024]{0:T(1024)S(1)} %pad_clamp_fusion.7), kind=kCustom, calls=%fused_computation.clone.1 | custom fusion | bytes 8388672 | tf_op jit(solution)/shard_map/while/body/eval_jaxpr/gather | solution.py:60
  83.2 3.6 %fusion.27 = bf16[1,16,2,128,128]{3,4,2,1,0:T(8,128)(2,1)S(1)} fusion(bf16[16,128,1024]{2,1,0:T(8,128)(2,1)} %gather_fusion, bf16[8,2,128,1024]{3,2,1,0:T(8,128)(2,1)} %get-tuple-element.101, s32[]{:T(128)} %get-tuple-element.91), kind=kOutput, calls=%fused_computation.8.clone.1 | convolution fusion | flops 1073741824 | bytes 5767680 | tf_op jit(solution)/shard_map/while/body/eval_jaxpr/sab,kcb->ksac/dot_general | solution.py:61
  88.6 4.9 %gather_fusion = bf16[16,128,1024]{2,1,0:T(8,128)(2,1)} fusion(bf16[16,128,1024]{2,1,0:T(8,128)(2,1)} %get-tuple-element.100, s32[1024]{0:T(1024)S(1)} %pad_clamp_fusion.7), kind=kCustom, calls=%fused_computation.clone.1 | custom fusion | bytes 8388672 | tf_op jit(solution)/shard_map/while/body/eval_jaxpr/gather | solution.py:60
  93.5 3.6 %fusion.27 = bf16[1,16,2,128,128]{3,4,2,1,0:T(8,128)(2,1)S(1)} fusion(bf16[16,128,1024]{2,1,0:T(8,128)(2,1)} %gather_fusion, bf16[8,2,128,1024]{3,2,1,0:T(8,128)(2,1)} %get-tuple-element.101, s32[]{:T(128)} %get-tuple-element.91), kind=kOutput, calls=%fused_computation.8.clone.1 | convolution fusion | flops 1073741824 | bytes 5767680 | tf_op jit(solution)/shard_map/while/body/eval_jaxpr/sab,kcb->ksac/dot_general | solution.py:61
  99.0 4.9 %gather_fusion = bf16[16,128,1024]{2,1,0:T(8,128)(2,1)} fusion(bf16[16,128,1024]{2,1,0:T(8,128)(2,1)} %get-tuple-element.100, s32[1024]{0:T(1024)S(1)} %pad_clamp_fusion.7), kind=kCustom, calls=%fused_computation.clone.1 | custom fusion | bytes 8388672 | tf_op jit(solution)/shard_map/while/body/eval_jaxpr/gather | solution.py:60
  103.9 3.6 %fusion.27 = bf16[1,16,2,128,128]{3,4,2,1,0:T(8,128)(2,1)S(1)} fusion(bf16[16,128,1024]{2,1,0:T(8,128)(2,1)} %gather_fusion, bf16[8,2,128,1024]{3,2,1,0:T(8,128)(2,1)} %get-tuple-element.101, s32[]{:T(128)} %get-tuple-element.91), kind=kOutput, calls=%fused_computation.8.clone.1 | convolution fusion | flops 1073741824 | bytes 5767680 | tf_op jit(solution)/shard_map/while/body/eval_jaxpr/sab,kcb->ksac/dot_general | solution.py:61
  109.3 4.9 %gather_fusion = bf16[16,128,1024]{2,1,0:T(8,128)(2,1)} fusion(bf16[16,128,1024]{2,1,0:T(8,128)(2,1)} %get-tuple-element.100, s32[1024]{0:T(1024)S(1)} %pad_clamp_fusion.7), kind=kCustom, calls=%fused_computation.clone.1 | custom fusion | bytes 8388672 | tf_op jit(solution)/shard_map/while/body/eval_jaxpr/gather | solution.py:60
  114.3 3.6 %fusion.27 = bf16[1,16,2,128,128]{3,4,2,1,0:T(8,128)(2,1)S(1)} fusion(bf16[16,128,1024]{2,1,0:T(8,128)(2,1)} %gather_fusion, bf16[8,2,128,1024]{3,2,1,0:T(8,128)(2,1)} %get-tuple-element.101, s32[]{:T(128)} %get-tuple-element.91), kind=kOutput, calls=%fused_computation.8.clone.1 | convolution fusion | flops 1073741824 | bytes 5767680 | tf_op jit(solution)/shard_map/while/body/eval_jaxpr/sab,kcb->ksac/dot_general | solution.py:61
  119.7 4.9 %gather_fusion = bf16[16,128,1024]{2,1,0:T(8,128)(2,1)} fusion(bf16[16,128,1024]{2,1,0:T(8,128)(2,1)} %get-tuple-element.100, s32[1024]{0:T(1024)S(1)} %pad_clamp_fusion.7), kind=kCustom, calls=%fused_computation.clone.1 | custom fusion | bytes 8388672 | tf_op jit(solution)/shard_map/while/body/eval_jaxpr/gather | solution.py:60
  124.6 3.6 %fusion.27 = bf16[1,16,2,128,128]{3,4,2,1,0:T(8,128)(2,1)S(1)} fusion(bf16[16,128,1024]{2,1,0:T(8,128)(2,1)} %gather_fusion, bf16[8,2,128,1024]{3,2,1,0:T(8,128)(2,1)} %get-tuple-element.101, s32[]{:T(128)} %get-tuple-element.91), kind=kOutput, calls=%fused_computation.8.clone.1 | convolution fusion | flops 1073741824 | bytes 5767680 | tf_op jit(solution)/shard_map/while/body/eval_jaxpr/sab,kcb->ksac/dot_general | solution.py:61
  130.1 4.9 %gather_fusion = bf16[16,128,1024]{2,1,0:T(8,128)(2,1)} fusion(bf16[16,128,1024]{2,1,0:T(8,128)(2,1)} %get-tuple-element.100, s32[1024]{0:T(1024)S(1)} %pad_clamp_fusion.7), kind=kCustom, calls=%fused_computation.clone.1 | custom fusion | bytes 8388672 | tf_op jit(solution)/shard_map/while/body/eval_jaxpr/gather | solution.py:60
  135.0 3.6 %fusion.27 = bf16[1,16,2,128,128]{3,4,2,1,0:T(8,128)(2,1)S(1)} fusion(bf16[16,128,1024]{2,1,0:T(8,128)(2,1)} %gather_fusion, bf16[8,2,128,1024]{3,2,1,0:T(8,128)(2,1)} %get-tuple-element.101, s32[]{:T(128)} %get-tuple-element.91), kind=kOutput, calls=%fused_computation.8.clone.1 | convolution fusion | flops 1073741824 | bytes 5767680 | tf_op jit(solution)/shard_map/while/body/eval_jaxpr/sab,kcb->ksac/dot_general | solution.py:61
  140.5 4.9 %gather_fusion = bf16[16,128,1024]{2,1,0:T(8,128)(2,1)} fusion(bf16[16,128,1024]{2,1,0:T(8,128)(2,1)} %get-tuple-element.100, s32[1024]{0:T(1024)S(1)} %pad_clamp_fusion.7), kind=kCustom, calls=%fused_computation.clone.1 | custom fusion | bytes 8388672 | tf_op jit(solution)/shard_map/while/body/eval_jaxpr/gather | solution.py:60
  145.4 3.6 %fusion.27 = bf16[1,16,2,128,128]{3,4,2,1,0:T(8,128)(2,1)S(1)} fusion(bf16[16,128,1024]{2,1,0:T(8,128)(2,1)} %gather_fusion, bf16[8,2,128,1024]{3,2,1,0:T(8,128)(2,1)} %get-tuple-element.101, s32[]{:T(128)} %get-tuple-element.91), kind=kOutput, calls=%fused_computation.8.clone.1 | convolution fusion | flops 1073741824 | bytes 5767680 | tf_op jit(solution)/shard_map/while/body/eval_jaxpr/sab,kcb->ksac/dot_general | solution.py:61
  150.8 4.9 %gather_fusion = bf16[16,128,1024]{2,1,0:T(8,128)(2,1)} fusion(bf16[16,128,1024]{2,1,0:T(8,128)(2,1)} %get-tuple-element.100, s32[1024]{0:T(1024)S(1)} %pad_clamp_fusion.7), kind=kCustom, calls=%fused_computation.clone.1 | custom fusion | bytes 8388672 | tf_op jit(solution)/shard_map/while/body/eval_jaxpr/gather | solution.py:60
  155.8 3.6 %fusion.27 = bf16[1,16,2,128,128]{3,4,2,1,0:T(8,128)(2,1)S(1)} fusion(bf16[16,128,1024]{2,1,0:T(8,128)(2,1)} %gather_fusion, bf16[8,2,128,1024]{3,2,1,0:T(8,128)(2,1)} %get-tuple-element.101, s32[]{:T(128)} %get-tuple-element.91), kind=kOutput, calls=%fused_computation.8.clone.1 | convolution fusion | flops 1073741824 | bytes 5767680 | tf_op jit(solution)/shard_map/while/body/eval_jaxpr/sab,kcb->ksac/dot_general | solution.py:61
  161.2 51.6 %reduce-scatter.2.cloned.1.call-done = bf16[8,16,2,16,128]{4,3,1,0,2:T(8,128)(2,1)} async-done(((bf16[8,16,2,128,128]{4,3,1,0,2:T(8,128)(2,1)}), bf16[8,16,2,16,128]{4,3,1,0,2:T(8,128)(2,1)}) %reduce-scatter.2.cloned.1.call-update) | async-done | bytes 1048592 | tf_op jit(solution)/shard_map/reduce_scatter | solution.py:64
  (90 shorter events, 39.2 us)
Async XLA Ops:
  7.2 205.6 %reduce-scatter.2.cloned.1.call-start = ((), (), s32[]{:S(2)}) async-start(), calls=%async_computation.1 | async-start | bytes 9437184 | tf_op jit(solution)/shard_map/reduce_scatter | solution.py:64
  8.9 19.8 %collective-permute-start = (s32[2]{0:T(128)S(1)}, s32[2]{0:T(128)S(1)}, u32[]{:S(2)}, u32[]{:S(2)}) collective-permute-start(s32[2]{0:T(128)S(1)} %get-tuple-element.33), channel_id=1, source_target_pairs={{0,240},{8,248},{16,0},{24,8},{32,16},{40,24},{48,32},{56,40},{64,... | collective-permute-start | bytes 32 | tf_op jit(solution)/shard_map/ppermute | solution.py:13
  17.3 11.4 %collective-permute-start.2 = (s32[2]{0:T(128)S(1)}, s32[2]{0:T(128)S(1)}, u32[]{:S(2)}, u32[]{:S(2)}) collective-permute-start(s32[2]{0:T(128)S(1)} %get-tuple-element.32), channel_id=1, source_target_pairs={{0,248},{8,0},{16,8},{24,16},{32,24},{40,32},{48,40},{56,48},{64,5... | collective-permute-start | bytes 32 | tf_op jit(solution)/shard_map/ppermute | solution.py:13
  18.5 13.1 %collective-permute-start.4 = (s32[2]{0:T(128)S(1)}, s32[2]{0:T(128)S(1)}, u32[]{:S(2)}, u32[]{:S(2)}) collective-permute-start(s32[2]{0:T(128)S(1)} %get-tuple-element.31), channel_id=1, source_target_pairs={{0,8},{8,16},{16,24},{24,32},{32,40},{40,48},{48,56},{56,64},{64,7... | collective-permute-start | bytes 32 | tf_op jit(solution)/shard_map/ppermute | solution.py:13
  19.3 12.2 %collective-permute-start.6 = (s32[2]{0:T(128)S(1)}, s32[2]{0:T(128)S(1)}, u32[]{:S(2)}, u32[]{:S(2)}) collective-permute-start(s32[2]{0:T(128)S(1)} %get-tuple-element.30), channel_id=1, source_target_pairs={{0,16},{8,24},{16,32},{24,40},{32,48},{40,56},{48,64},{56,72},{64,... | collective-permute-start | bytes 32 | tf_op jit(solution)/shard_map/ppermute | solution.py:13
  26.4 2.4 %copy-start.1 = (bf16[1024,1024]{1,0:T(8,128)(2,1)S(1)}, bf16[1024,1024]{1,0:T(8,128)(2,1)}, u32[]{:S(2)}) copy-start(bf16[1024,1024]{1,0:T(8,128)(2,1)} %param.6) | copy-start | bytes 6291460
  30.1 18.5 %collective-permute-start.1 = (bf16[2,128,1024]{2,1,0:T(8,128)(2,1)}, bf16[2,128,1024]{2,1,0:T(8,128)(2,1)S(1)}, u32[]{:S(2)}, u32[]{:S(2)}) collective-permute-start(bf16[2,128,1024]{2,1,0:T(8,128)(2,1)} %gather_fusion.2), channel_id=1, source_target_pairs={{0,16},{8,24},{16,32},{24,40},{32,48},{40,56},{48,64},{56,72},{64,... | collective-permute-start | bytes 1572872 | tf_op jit(solution)/shard_map/ppermute | solution.py:13
  31.5 28.0 %collective-permute-start.3 = (bf16[2,128,1024]{2,1,0:T(8,128)(2,1)}, bf16[2,128,1024]{2,1,0:T(8,128)(2,1)S(1)}, u32[]{:S(2)}, u32[]{:S(2)}) collective-permute-start(bf16[2,128,1024]{2,1,0:T(8,128)(2,1)} %gather_fusion.3), channel_id=1, source_target_pairs={{0,8},{8,16},{16,24},{24,32},{32,40},{40,48},{48,56},{56,64},{64,7... | collective-permute-start | bytes 1572872 | tf_op jit(solution)/shard_map/ppermute | solution.py:13
  33.0 42.2 %collective-permute-start.5 = (bf16[2,128,1024]{2,1,0:T(8,128)(2,1)}, bf16[2,128,1024]{2,1,0:T(8,128)(2,1)}, u32[]{:S(2)}, u32[]{:S(2)}) collective-permute-start(bf16[2,128,1024]{2,1,0:T(8,128)(2,1)} %gather_fusion.4), channel_id=1, source_target_pairs={{0,248},{8,0},{16,8},{24,16},{32,24},{40,32},{48,40},{56,48},{64,5... | collective-permute-start | bytes 1572872 | tf_op jit(solution)/shard_map/ppermute | solution.py:13
  39.7 36.6 %collective-permute-start.7 = (bf16[2,128,1024]{2,1,0:T(8,128)(2,1)}, bf16[2,128,1024]{2,1,0:T(8,128)(2,1)S(1)}, u32[]{:S(2)}, u32[]{:S(2)}) collective-permute-start(bf16[2,128,1024]{2,1,0:T(8,128)(2,1)} %gather_fusion.5), channel_id=1, source_target_pairs={{0,240},{8,248},{16,0},{24,8},{32,16},{40,24},{48,32},{56,40},{64,... | collective-permute-start | bytes 1572872 | tf_op jit(solution)/shard_map/ppermute | solution.py:13
  76.3 2.0 copy-start
Sparse Core Ops, SparseCore 0:
  161.3 51.4 reduce-scatter.1
where the time goes:
time: 226 us; the launch traced here: 223 us
  waiting for transfers between devices  84.5 us (37%)
  local copies, waits for them, and re-layouts  67.8 us (30%)
  matrix products  28.7 us (13%)
  starting transfers between devices  18.8 us (8%)
  between operations  14.3 us (6%)
  other arithmetic  8.3 us (4%)
    reduce_scatter x1, waiting for transfers between devices, body(): lax.psum_scatter(partial_value.astype(jnp.bfloat16), 'bands', scatter_dim...  51.6 us
    gather x8, local copies, waits for them, and re-layouts, one_block(): right = available[where_rows]  39.4 us
    ppermute x8, waiting for transfers between devices, shifted(): return lax.ppermute(value, axis, pairs)  32.9 us
    dot_general x8, matrix products, one_block(): jnp.einsum('sab,kcb->ksac', left, right, preferred_element_type=jnp.float32)  28.7 us
    ppermute x8, starting transfers between devices, shifted(): return lax.ppermute(value, axis, pairs)  18.7 us
    dynamic_update_slice x16, local copies, waits for them, and re-layouts, body(): partial_value = lax.map(one_block, (scaled, positions))  14.5 us
    gather x4, local copies, waits for them, and re-layouts, deliver(): return shifted(local_rows[asked], 'atoms', -offset)  5.51 us
  transfers between devices with their start and end apart: 9, of which 4 were waited for; matrix products, arithmetic and copies ran while one was open for 7% of the time, Pallas kernels for 0%

commit v1 on v0

v1 whole, which is shorter than its diff:
```python
import functools

import jax
import jax.numpy as jnp
from jax import lax
from jax.experimental import pallas as pl
from jax.experimental.pallas import tpu as pltpu
from jax.sharding import PartitionSpec as P

F32 = jnp.float32
BF16 = jnp.bfloat16
MESH = pl.DeviceIdType.MESH
CORES = 2
PAIR = 2


def exchange_kernel(
    eig, occ, en, neigh,
    tiles_out, pos_out,
    own, mate, far, lhs, vec, ybuf, r1, fbuf, gbuf, s2, send, relay, req_out, req_in, neigh_v, pos_v, tiles,
    ld_sem, own_send, own_recv, vec_send, vec_recv, req_send, req_recv,
    x_send, x_recv, fwd_send, fwd_recv, y_send, y_recv, out_sem,
):
    n = lax.axis_size("atoms")
    d = lax.axis_index("atoms")
    band = lax.axis_index("bands")
    bands = lax.axis_size("bands")
    ny = bands // CORES
    y = band // CORES
    c = lax.rem(band, CORES)
    blocks = neigh.shape[0]
    tile = eig.shape[1]
    keep = tile // bands
    stages = ybuf.shape[0]
    own_stages = blocks // PAIR
    wide = PAIR * tile
    group = blocks * keep

    def at_domain(step):
        return (lax.rem(d + step + n, n), band)

    def at_y(step):
        return (d, lax.rem(y + step + ny, ny) * CORES + c)

    partner = (d, y * CORES + 1 - c)
    x_to = (at_domain(1), at_domain(-1))
    y_to = (at_y(1), at_y(-1))
    peers = [at_domain(s) for s in (1, -1, 2, -2)] + [y_to[0], y_to[1], partner]

    barrier = pltpu.get_barrier_semaphore()
    for peer in peers:
        pl.semaphore_signal(barrier, inc=1, device_id=peer, device_id_type=MESH)

    load_ids = pltpu.make_async_copy(neigh, neigh_v, ld_sem.at[0])
    load_occ = pltpu.make_async_copy(occ, vec.at[0, 0], ld_sem.at[1])
    load_en = pltpu.make_async_copy(en, vec.at[0, 1], ld_sem.at[2])
    load_eig = pltpu.make_async_copy(eig, own, ld_sem.at[3])
    load_ids.start()
    load_occ.start()
    load_en.start()
    load_eig.start()

    load_ids.wait()
    ids = neigh_v[...]
    shift = blocks.bit_length() - 1
    owner = lax.shift_right_logical(ids, jnp.full_like(ids, shift))
    within = ids & (blocks - 1)
    pos = within
    row = lax.broadcasted_iota(jnp.int32, req_out.shape[1:], 0)
    steps = (-1, 1, -2, 2)
    for q, step in enumerate(steps):
        mask = owner == lax.rem(d + step + n, n)
        low = jnp.min(jnp.where(mask, within, blocks - 1))
        high = jnp.max(jnp.where(mask, within, 0))
        req_out[q] = jnp.where(row == 0, low, high)
        base = blocks + 4 * (q // 2) + q % 2
        pos = jnp.where(mask, base + 2 * (within != low).astype(jnp.int32), pos)
    pos_v[...] = pos
    put_pos = pltpu.make_async_copy(pos_v, pos_out, out_sem.at[stages])
    put_pos.start()

    def remote(src, dst, s_sem, r_sem, to):
        return pltpu.make_async_remote_copy(
            src_ref=src, dst_ref=dst, send_sem=s_sem, recv_sem=r_sem,
            device_id=to, device_id_type=MESH,
        )

    pl.semaphore_wait(barrier, len(peers))

    asks = [
        remote(req_out.at[q], req_in.at[q], req_send.at[q], req_recv.at[q], at_domain(step))
        for q, step in enumerate(steps)
    ]
    for ask in asks:
        ask.start()
    swaps = [
        remote(occ, vec.at[1, 0], vec_send.at[0], vec_recv.at[0], partner),
        remote(en, vec.at[1, 1], vec_send.at[1], vec_recv.at[1], partner),
    ]
    for s in range(own_stages):
        rows = pl.ds(s * PAIR, PAIR)
        swaps.append(
            remote(eig.at[rows], mate.at[rows], own_send.at[s], own_recv.at[s], partner)
        )
    for swap in swaps:
        swap.start()

    def scale(kc, source):
        first = vec[kc, 0]
        second = first * vec[kc, 1]

        def step(t, carry):
            rel = t // blocks
            i = lax.rem(t, blocks)
            dest = lax.rem(y + rel, ny)
            at = pl.multiple_of((dest * CORES + c) * keep, keep)
            x = source[i, pl.ds(at, keep), :].astype(F32)
            to = pl.multiple_of(rel * 2 * group + i * keep, keep)
            lhs[kc, pl.ds(to, keep), :] = (x * first).astype(BF16)
            to = pl.multiple_of(rel * 2 * group + group + i * keep, keep)
            lhs[kc, pl.ds(to, keep), :] = (x * second).astype(BF16)
            return carry

        lax.fori_loop(0, ny * blocks, step, 0)

    load_occ.wait()
    load_en.wait()
    load_eig.wait()
    scale(0, own)

    for ask in asks:
        ask.wait_recv()
    hops = {}
    for rank in range(2):
        for side in range(2):
            for kind in range(2):
                q = 2 * kind + side
                b = jnp.max(req_in[q, rank:rank + 1, :])
                send[2 * q + rank] = own[b]
    for rank in range(2):
        for kind in range(2):
            for side in range(2):
                q = 2 * kind + side
                dst = far.at[0, 2 * rank + side] if kind == 0 else relay.at[2 * rank + side]
                hop = remote(
                    send.at[2 * q + rank], dst,
                    x_send.at[kind, rank, side], x_recv.at[kind, rank, side], x_to[side],
                )
                hop.start()
                hops[kind, rank, side] = hop

    for swap in swaps:
        swap.wait_recv()
    scale(1, mate)

    def multiply(s):
        if s < own_stages:
            right = [blk[pl.ds(s * PAIR, PAIR)].reshape(wide, -1) for blk in (own, mate)]
        else:
            right = [far[k, pl.ds((s - own_stages) * PAIR, PAIR)].reshape(wide, -1) for k in range(CORES)]
        half = lhs.shape[1] // 2
        dims = (((1,), (1,)), ((), ()))

        def step(m, carry):
            rows = pl.ds(pl.multiple_of(m * half, half), half)
            total = lax.dot_general(lhs[0, rows, :], right[0], dims, preferred_element_type=F32)
            total += lax.dot_general(lhs[1, rows, :], right[1], dims, preferred_element_type=F32)
            ybuf[s, rows, :] = total.astype(BF16)
            return carry

        lax.fori_loop(0, 2, step, 0)

    def piece(s, rel, which):
        return ybuf.at[s, pl.ds((2 * rel + which) * group, group), :]

    y_hops = {}

    def first_sends(s):
        plan = (
            (piece(s, 2, 0), r1.at[s, 0], 0),
            (piece(s, 2, 1), r1.at[s, 1], 1),
            (piece(s, 1, 1), fbuf.at[s, 1], 0),
            (piece(s, 3, 0), fbuf.at[s, 0], 1),
        )
        for k, (src, dst, side) in enumerate(plan):
            y_hops[s, k] = remote(src, dst, y_send.at[s, k], y_recv.at[s, k], y_to[side])
            y_hops[s, k].start()

    def second_sends(s):
        for which in range(2):
            y_hops[s, which].wait_recv()
            rel = 1 if which == 0 else 3
            s2[s, which] = (r1[s, which].astype(F32) + piece(s, rel, which)[...].astype(F32)).astype(BF16)
            y_hops[s, 4 + which] = remote(
                s2.at[s, which], gbuf.at[s, which], y_send.at[s, 4 + which], y_recv.at[s, 4 + which], y_to[which],
            )
            y_hops[s, 4 + which].start()

    puts = []

    def finish(s):
        for k in (2, 3, 4, 5):
            y_hops[s, k].wait_recv()
        for which in range(2):
            total = piece(s, 0, which)[...].astype(F32) + fbuf[s, which].astype(F32) + gbuf[s, which].astype(F32)
            for jj in range(PAIR):
                tiles[which, PAIR * s + jj] = total[:, jj * tile:(jj + 1) * tile]
        blk = pl.ds(PAIR * s, PAIR)
        put = pltpu.make_async_copy(tiles.at[:, blk], tiles_out.at[:, blk], out_sem.at[s])
        put.start()
        puts.append(put)

    forwards = {}

    def forward(kind, rank):
        for side in range(2):
            hops[kind, rank, side].wait_recv()
            k = 2 * kind + 2 * rank + side
            forwards[k] = remote(
                far.at[0, k], far.at[1, k], fwd_send.at[k], fwd_recv.at[k], partner
            )
            forwards[k].start()

    def pass_on(rank):
        for side in range(2):
            hops[1, rank, side].wait_recv()
            hop = remote(
                relay.at[2 * rank + side], far.at[0, 4 + 2 * rank + side],
                x_send.at[2, rank, side], x_recv.at[2, rank, side], x_to[side],
            )
            hop.start()
            hops[2, rank, side] = hop

    def remote_stage(s):
        for side in range(2):
            forwards[PAIR * (s - own_stages) + side].wait_recv()
        multiply(s)
        first_sends(s)

    for s in range(own_stages):
        multiply(s)
        first_sends(s)
    second_sends(0)
    forward(0, 0)
    second_sends(1)
    remote_stage(4)
    second_sends(2)
    pass_on(0)
    second_sends(3)
    forward(0, 1)
    second_sends(4)
    remote_stage(5)
    finish(0)
    finish(1)
    finish(2)
    pass_on(1)
    finish(3)
    finish(4)
    second_sends(5)
    forward(2, 0)
    remote_stage(6)
    finish(5)
    second_sends(6)
    forward(2, 1)
    remote_stage(7)
    finish(6)
    second_sends(7)
    finish(7)

    for copy in asks + swaps + list(hops.values()) + list(forwards.values()) + list(y_hops.values()):
        copy.wait_send()
    put_pos.wait()
    for put in puts:
        put.wait()


def place_kernel(pos, tiles, density, energy):
    per, slots = density.shape[:2]
    first = pl.program_id(0) * per
    for i in range(per):
        for k in range(slots):
            p = pos[first + i, k]
            density[i, k] = tiles[0, p, i]
            energy[i, k] = tiles[1, p, i]


def body(eigvecs, occupations, energies, neighbours):
    bands = lax.axis_size("bands")
    blocks, slots = neighbours.shape
    rows, depth = eigvecs.shape
    tile = rows // blocks
    keep = tile // bands
    group = blocks * keep
    ny = bands // CORES
    pool_blocks = blocks + 8
    stages = pool_blocks // PAIR
    wide = PAIR * tile
    any_space = pl.BlockSpec(memory_space=pl.ANY)
    dma = pltpu.SemaphoreType.DMA
    tiles, pos = pl.pallas_call(
        exchange_kernel,
        out_shape=(
            jax.ShapeDtypeStruct((2, pool_blocks, group, tile), F32),
            jax.ShapeDtypeStruct((blocks, slots), jnp.int32),
        ),
        in_specs=[any_space] * 4,
        out_specs=(any_space, any_space),
        scratch_shapes=[
            pltpu.VMEM((blocks, tile, depth), BF16),
            pltpu.VMEM((blocks, tile, depth), BF16),
            pltpu.VMEM((CORES, 8, tile, depth), BF16),
            pltpu.VMEM((CORES, ny * 2 * group, depth), BF16),
            pltpu.VMEM((CORES, 2, 1, depth), F32),
            pltpu.VMEM((stages, ny * 2 * group, wide), BF16),
            pltpu.VMEM((stages, 2, group, wide), BF16),
            pltpu.VMEM((stages, 2, group, wide), BF16),
            pltpu.VMEM((stages, 2, group, wide), BF16),
            pltpu.VMEM((stages, 2, group, wide), BF16),
            pltpu.VMEM((8, tile, depth), BF16),
            pltpu.VMEM((4, tile, depth), BF16),
            pltpu.VMEM((4, 8, 128), jnp.int32),
            pltpu.VMEM((4, 8, 128), jnp.int32),
            pltpu.VMEM((blocks, slots), jnp.int32),
            pltpu.VMEM((blocks, slots), jnp.int32),
            pltpu.VMEM((2, pool_blocks, group, tile), F32),
            dma((4,)),
            dma((blocks // PAIR,)),
            dma((blocks // PAIR,)),
            dma((2,)),
            dma((2,)),
            dma((4,)),
            dma((4,)),
            dma((3, 2, 2)),
            dma((3, 2, 2)),
            dma((8,)),
            dma((8,)),
            dma((stages, 6)),
            dma((stages, 6)),
            dma((stages + 1,)),
        ],
        compiler_params=pltpu.CompilerParams(
            collective_id=0, has_side_effects=True, vmem_limit_bytes=60 * 2**20
        ),
        name="exchange",
    )(eigvecs.reshape(blocks, tile, depth), occupations.reshape(1, depth), energies.reshape(1, depth), neighbours)
    tiles = tiles.reshape(2, pool_blocks, blocks, keep, tile)
    per = 2
    out = jax.ShapeDtypeStruct((blocks, slots, keep, tile), F32)
    density, energy = pl.pallas_call(
        place_kernel,
        out_shape=(out, out),
        grid_spec=pltpu.PrefetchScalarGridSpec(
            num_scalar_prefetch=1,
            grid=(blocks // per,),
            in_specs=[pl.BlockSpec((2, pool_blocks, per, keep, tile), lambda i, pos: (0, 0, i, 0, 0))],
            out_specs=[pl.BlockSpec((per, slots, keep, tile), lambda i, pos: (i, 0, 0, 0))] * 2,
        ),
        name="place",
    )(pos, tiles)
    return density, energy


def solution(mesh):
    return jax.shard_map(
        body,
        mesh=mesh,
        in_specs=(P("atoms", "bands"), P("bands"), P("bands"), P("atoms", None)),
        out_specs=(P("atoms", None, "bands", None), P("atoms", None, "bands", None)),
        check_vma=False,
    )
```

time: 226 us -> 70 us (0.31); the launches traced: 223 us -> 69.5 us
  waiting for transfers between devices: 84.5 us -> 0 us
  Pallas kernels: 0 us -> 68.9 us
  local copies, waits for them, and re-layouts: 67.8 us -> 0 us
  matrix products: 28.7 us -> 0 us
  starting transfers between devices: 18.8 us -> 0 us
  between operations: 14.3 us -> 0.64 us
  other arithmetic: 8.3 us -> 0 us
    pallas_call x0 -> x2, Pallas kernels: none -> 68.9 us  [the longest x1 64.4 us: body(): pl.pallas_call(exchange_kernel, out_shape=(jax.ShapeDtypeStruct((2, pool_...]
    reduce_scatter x1 -> x0, waiting for transfers between devices: 51.6 us -> none  [body(): lax.psum_scatter(partial_value.astype(jnp.bfloat16), 'bands', scatter_dim...]
    gather x14 -> x0, local copies, waits for them, and re-layouts: 46.2 us -> none  [the longest x8 39.4 us: one_block(): right = available[where_rows]]
    ppermute x8 -> x0, waiting for transfers between devices: 32.9 us -> none  [shifted(): return lax.ppermute(value, axis, pairs)]
    dot_general x8 -> x0, matrix products: 28.7 us -> none  [one_block(): jnp.einsum('sab,kcb->ksac', left, right, preferred_element_type=jnp.float32)]
    ppermute x8 -> x0, starting transfers between devices: 18.7 us -> none  [shifted(): return lax.ppermute(value, axis, pairs)]
    dynamic_update_slice x16 -> x0, local copies, waits for them, and re-layouts: 14.5 us -> none  [body(): partial_value = lax.map(one_block, (scaled, positions))]
    another operation x3 -> x0, other arithmetic: 5.05 us -> none
  transfers between devices with their start and end apart: 9 -> 0, of which waited for: 4 -> 0; matrix products, arithmetic and copies ran while one was open for 7% -> 0% of each run, Pallas kernels for 0% -> 0%
where the time goes in v1:
time: 70 us; the launch traced here: 69.5 us
  Pallas kernels  68.9 us (98%)
    pallas_call x1, Pallas kernels, body(): pl.pallas_call(exchange_kernel, out_shape=(jax.ShapeDtypeStruct((2, pool_...  64.4 us
    pallas_call x1, Pallas kernels, body(): pl.pallas_call(place_kernel, out_shape=(out, out), grid_spec=pltpu.Prefet...  4.51 us

profile of v1, /device:TPU:8, one launch (start us, length us, event | category | flops | bytes accessed | tf_op | source)
XLA Modules:
  0.0 69.5 jit_solution(14266665709690211089)
XLA Ops:
  0.6 64.4 %exchange.1 = (f32[2,16,128,128]{3,2,1,0:T(8,128)}, s32[8,16]{1,0:T(8,128)}) custom-call(bf16[8,128,1024]{2,1,0:T(8,128)(2,1)} %bitcast.4, f32[1,1024]{1,0:T(1,128)} %bitcast.6, f32[1,1024]{1,0:T(1,128)} %bitcast.7, s32[8,16]{1,0:T(8,128)} %neigh.1), custom_call_target="tpu_custom_call" | custom-call | tf_op jit(solution)/shard_map/exchange/pallas_call | solution.py:300
  65.0 4.5 %place.1 = (f32[8,16,16,128]{3,2,1,0:T(8,128)}, f32[8,16,16,128]{3,2,1,0:T(8,128)}) custom-call(s32[8,16]{1,0:T(8,128)} %get-tuple-element.4.pos, f32[2,16,8,16,128]{4,3,2,1,0:T(8,128)} %bitcast.5), custom_call_target="tpu_custom_call" | custom-call | tf_op jit(solution)/shard_map/place/pallas_call | solution.py:349

commit v2 on v1

v2 whole, which is shorter than its diff:
```python
import jax
import jax.numpy as jnp
from jax import lax
from jax.experimental import pallas as pl
from jax.experimental.pallas import tpu as pltpu
from jax.sharding import PartitionSpec as P

F32 = jnp.float32
BF16 = jnp.bfloat16
MESH = pl.DeviceIdType.MESH
CORES = 2
PAIR = 2
WHOLE = 6
HALVES = 4
FAR = 8
ORDER = (2, 1, 3, 0)


def exchange_kernel(
    eig, occ, en, neigh,
    tiles, pos_out,
    own, mate, far, lhs, vec,
    y_whole, rx_whole, y_half, rx_half,
    send, relay, req_out, req_in, neigh_v, pos_v,
    ld_sem, own_send, own_recv, vec_send, vec_recv, req_send, req_recv,
    x_send, x_recv, b_send, b_recv, fc_send, fc_recv, fb_send, fb_recv,
    yw_send, yw_recv, yh_send, yh_recv, out_sem,
):
    n = lax.axis_size("atoms")
    d = lax.axis_index("atoms")
    band = lax.axis_index("bands")
    y = band // CORES
    c = lax.rem(band, CORES)
    blocks, ny, _, keep, depth = eig.shape
    group = blocks * keep
    tile = ny * CORES * keep
    own_stages = blocks // PAIR

    def at_domain(step):
        return (lax.rem(d + step + n, n), band)

    def at_y(step):
        return (d, lax.rem(y + step + ny, ny) * CORES + c)

    partner = (d, y * CORES + 1 - c)
    x_to = (at_domain(1), at_domain(-1))
    y_to = (at_y(1), at_y(-1))
    peers = [at_domain(s) for s in (2, -2, 1, -1)] + [y_to[0], y_to[1], partner]

    barrier = pltpu.get_barrier_semaphore()
    for peer in peers:
        pl.semaphore_signal(barrier, inc=1, device_id=peer, device_id_type=MESH)

    load_ids = pltpu.make_async_copy(neigh, neigh_v, ld_sem.at[0])
    load_occ = pltpu.make_async_copy(occ, vec.at[0, 0], ld_sem.at[1])
    load_en = pltpu.make_async_copy(en, vec.at[0, 1], ld_sem.at[2])
    load_eig = pltpu.make_async_copy(eig, own, ld_sem.at[3])
    load_ids.start()
    load_eig.start()
    load_occ.start()
    load_en.start()

    load_ids.wait()
    ids = neigh_v[...]
    shift = blocks.bit_length() - 1
    owner = lax.shift_right_logical(ids, jnp.full_like(ids, shift))
    within = ids & (blocks - 1)
    row = lax.broadcasted_iota(jnp.int32, req_out.shape[1:], 0)
    steps = (-1, 1, -2, 2)
    masks, lows = [], []
    for q, step in enumerate(steps):
        mask = owner == lax.rem(d + step + n, n)
        low = jnp.min(jnp.where(mask, within, blocks - 1))
        high = jnp.max(jnp.where(mask, within, 0))
        req_out[q] = jnp.where(row == 0, low, high)
        masks.append(mask)
        lows.append(low)

    def remote(src, dst, s_sem, r_sem, to):
        return pltpu.make_async_remote_copy(
            src_ref=src, dst_ref=dst, send_sem=s_sem, recv_sem=r_sem,
            device_id=to, device_id_type=MESH,
        )

    pl.semaphore_wait(barrier, len(peers))

    asks = [
        remote(req_out.at[q], req_in.at[q], req_send.at[q], req_recv.at[q], at_domain(step))
        for q, step in enumerate(steps)
    ]
    swaps = [
        remote(occ, vec.at[1, 0], vec_send.at[0], vec_recv.at[0], partner),
        remote(en, vec.at[1, 1], vec_send.at[1], vec_recv.at[1], partner),
        remote(eig.at[:, :, 1 - c], mate.at[:, :, 1 - c], own_send.at[own_stages], own_recv.at[own_stages], partner),
    ]
    for s in range(own_stages):
        blk = pl.ds(s * PAIR, PAIR)
        swaps.append(remote(eig.at[blk, :, c], mate.at[blk, :, c], own_send.at[s], own_recv.at[s], partner))
    for copy in asks + swaps:
        copy.start()

    pos = within
    for q in range(4):
        base = blocks + 4 * (q // 2) + q % 2
        pos = jnp.where(masks[q], base + 2 * (within != lows[q]).astype(jnp.int32), pos)
    pos_v[...] = pos
    put_pos = pltpu.make_async_copy(pos_v, pos_out, out_sem.at[0])
    put_pos.start()

    def scale(kc, source):
        first = vec[kc, 0]
        second = first * vec[kc, 1]
        for k, rel in enumerate(ORDER):
            dest = lax.rem(y + rel, ny)

            def step(i, carry, k=k, dest=dest):
                x = source[i, dest, c].astype(F32)
                at = pl.multiple_of(2 * k * group + i * keep, keep)
                lhs[kc, pl.ds(at, keep), :] = (x * first).astype(BF16)
                at = pl.multiple_of((2 * k + 1) * group + i * keep, keep)
                lhs[kc, pl.ds(at, keep), :] = (x * second).astype(BF16)
                return carry

            lax.fori_loop(0, blocks, step, 0)

    load_occ.wait()
    load_en.wait()
    load_eig.wait()
    scale(0, own)

    hops = {}
    for rank in range(2):
        for kind in range(2):
            for side in range(2):
                q = 2 * kind + side
                if rank == 0:
                    asks[q].wait_recv()
                b = jnp.max(req_in[q, rank:rank + 1, :])
                send[2 * q + rank] = own[b]
            for side in range(2):
                q = 2 * kind + side
                dst = far.at[0, 2 * rank + side] if kind == 0 else relay.at[2 * rank + side]
                hops[kind, rank, side] = remote(
                    send.at[2 * q + rank], dst,
                    x_send.at[kind, rank, side], x_recv.at[kind, rank, side], x_to[side],
                )
                hops[kind, rank, side].start()

    for swap in swaps[:3]:
        swap.wait_recv()
    scale(1, mate)

    y_hops = {}
    dims = (((1,), (1,)), ((), ()))

    class Stage:
        def __init__(self, s):
            self.s = s
            if s < WHOLE:
                self.out, self.rx = y_whole.at[s], rx_whole.at[s]
                self.y_send, self.y_recv = yw_send.at[s], yw_recv.at[s]
            else:
                self.out, self.rx = y_half.at[s - WHOLE], rx_half.at[s - WHOLE]
                self.y_send, self.y_recv = yh_send.at[s - WHOLE], yh_recv.at[s - WHOLE]

        def right(self, k):
            s = self.s
            if s < own_stages:
                value = (own, mate)[k][pl.ds(s * PAIR, PAIR)]
            elif s < WHOLE:
                value = far[k, pl.ds((s - own_stages) * PAIR, PAIR)]
            else:
                rank, half = (s - WHOLE) // 2, (s - WHOLE) % 2
                value = far[k, pl.ds(4 + 2 * rank, PAIR), pl.ds(half * (ny // 2), ny // 2)]
            return value.reshape(-1, depth)

        def piece(self, rel, which):
            return self.out.at[pl.ds((2 * ORDER.index(rel) + which) * group, group), :]

        def rows(self, first, count):
            rows = pl.ds(first * group, count * group)
            total = lax.dot_general(lhs[0, rows, :], self.right(0), dims, preferred_element_type=F32)
            total += lax.dot_general(lhs[1, rows, :], self.right(1), dims, preferred_element_type=F32)
            self.out[rows, :] = total.astype(BF16)

        def hop(self, k, src, side):
            copy = remote(src, self.rx.at[k], self.y_send.at[k], self.y_recv.at[k], y_to[side])
            copy.start()
            y_hops[self.s, k] = copy

        def run(self):
            self.rows(0, 2)
            self.hop(0, self.piece(2, 0), 0)
            self.hop(1, self.piece(2, 1), 1)
            self.rows(2, 4)
            self.hop(3, self.piece(1, 1), 0)
            self.hop(2, self.piece(3, 0), 1)
            self.rows(6, 2)

        def relay(self):
            for which in range(2):
                y_hops[self.s, which].wait_recv()
                part = self.piece((1, 3)[which], which)
                self.rx[6 + which] = (self.rx[which].astype(F32) + part[...].astype(F32)).astype(BF16)
                self.hop(4 + which, self.rx.at[6 + which], which)

        def total(self, which):
            y_hops[self.s, 2 + which].wait_recv()
            y_hops[self.s, 4 + which].wait_recv()
            part = self.piece(0, which)[...].astype(F32)
            return part + self.rx[2 + which].astype(F32) + self.rx[4 + which].astype(F32)

    stages = [Stage(s) for s in range(WHOLE + HALVES)]

    def finish(s):
        for which in range(2):
            total = stages[s].total(which)
            for jj in range(PAIR):
                tiles[which, PAIR * s + jj] = total[:, jj * tile:(jj + 1) * tile]

    def finish_halves(rank):
        s = WHOLE + 2 * rank
        j = blocks + 4 + 2 * rank
        for which in range(2):
            one, two = stages[s].total(which), stages[s + 1].total(which)
            low = lax.broadcasted_iota(jnp.int32, one.shape, 1) < tile // 2
            tiles[which, j] = jnp.where(low, one, pltpu.roll(two, tile // 2, 1))
            tiles[which, j + 1] = jnp.where(low, pltpu.roll(one, tile // 2, 1), two)

    forwards = {}

    def forward(rank):
        for side in range(2):
            hops[0, rank, side].wait_recv()
            k = 2 * rank + side
            copy = remote(far.at[0, k], far.at[1, k], fc_send.at[k], fc_recv.at[k], partner)
            copy.start()
            forwards[own_stages + rank, side] = copy

    def far_piece(slot, rank, half, side):
        return far.at[slot, 4 + 2 * rank + side, pl.ds(half * (ny // 2), ny // 2)]

    def forward_half(rank, half):
        for side in range(2):
            hops[2, rank, half, side].wait_recv()
            copy = remote(
                far_piece(0, rank, half, side), far_piece(1, rank, half, side),
                fb_send.at[rank, half, side], fb_recv.at[rank, half, side], partner,
            )
            copy.start()
            forwards[WHOLE + 2 * rank + half, side] = copy

    def pass_on(rank):
        for half in range(2):
            for side in range(2):
                if half == 0:
                    hops[1, rank, side].wait_recv()
                copy = remote(
                    relay.at[2 * rank + side, pl.ds(half * (ny // 2), ny // 2)], far_piece(0, rank, half, side),
                    b_send.at[rank, half, side], b_recv.at[rank, half, side], x_to[side],
                )
                copy.start()
                hops[2, rank, half, side] = copy

    def run_far(s):
        for side in range(2):
            forwards[s, side].wait_recv()
        stages[s].run()

    for s in range(own_stages):
        swaps[3 + s].wait_recv()
        stages[s].run()
    forward(0)
    stages[0].relay()
    stages[1].relay()
    run_far(4)
    stages[2].relay()
    pass_on(0)
    stages[3].relay()
    forward(1)
    stages[4].relay()
    run_far(5)
    finish(0)
    finish(1)
    finish(2)
    pass_on(1)
    finish(3)
    stages[5].relay()
    forward_half(0, 0)
    finish(4)
    run_far(6)
    forward_half(0, 1)
    run_far(7)
    finish(5)
    stages[6].relay()
    forward_half(1, 0)
    run_far(8)
    stages[7].relay()
    forward_half(1, 1)
    run_far(9)
    finish_halves(0)
    stages[8].relay()
    stages[9].relay()
    finish_halves(1)

    for copy in asks + swaps + list(hops.values()) + list(forwards.values()) + list(y_hops.values()):
        copy.wait_send()
    put_pos.wait()


def place_kernel(pos, tiles, density, energy):
    per, slots, keep, _ = density.shape
    first = pl.program_id(0) * per
    for i in range(per):
        rows = pl.ds(pl.multiple_of((first + i) * keep, keep), keep)
        for k in range(slots):
            p = pos[first + i, k]
            density[i, k] = tiles[0, p, rows, :]
            energy[i, k] = tiles[1, p, rows, :]


def body(eigvecs, occupations, energies, neighbours):
    bands = lax.axis_size("bands")
    blocks, slots = neighbours.shape
    rows, depth = eigvecs.shape
    tile = rows // blocks
    keep = tile // bands
    group = blocks * keep
    ny = bands // CORES
    wide = PAIR * tile
    block = (ny, CORES, keep, depth)
    any_space = pl.BlockSpec(memory_space=pl.ANY)
    dma = pltpu.SemaphoreType.DMA
    sems = []
    for shape in (
        (blocks // PAIR + 1,), (2,), (4,), (2, 2, 2), (2, 2, 2), (4,), (2, 2, 2), (WHOLE, 6), (HALVES, 6),
    ):
        sems += [dma(shape), dma(shape)]
    tiles, pos = pl.pallas_call(
        exchange_kernel,
        out_shape=(
            pltpu.VMEM((2, blocks + FAR, group, tile), F32),
            pltpu.SMEM((blocks, slots), jnp.int32),
        ),
        in_specs=[any_space] * 4,
        out_specs=(pl.BlockSpec(memory_space=pltpu.VMEM), pl.BlockSpec(memory_space=pltpu.SMEM)),
        scratch_shapes=[
            pltpu.VMEM((blocks, *block), BF16),
            pltpu.VMEM((blocks, *block), BF16),
            pltpu.VMEM((CORES, FAR, *block), BF16),
            pltpu.VMEM((CORES, ny * 2 * group, depth), BF16),
            pltpu.VMEM((CORES, 2, 1, depth), F32),
            pltpu.VMEM((WHOLE, ny * 2 * group, wide), BF16),
            pltpu.VMEM((WHOLE, 8, group, wide), BF16),
            pltpu.VMEM((HALVES, ny * 2 * group, wide // 2), BF16),
            pltpu.VMEM((HALVES, 8, group, wide // 2), BF16),
            pltpu.VMEM((FAR, *block), BF16),
            pltpu.VMEM((4, *block), BF16),
            pltpu.VMEM((4, 8, 128), jnp.int32),
            pltpu.VMEM((4, 8, 128), jnp.int32),
            pltpu.VMEM((blocks, slots), jnp.int32),
            pltpu.VMEM((blocks, slots), jnp.int32),
            dma((4,)),
            *sems,
            dma((1,)),
        ],
        compiler_params=pltpu.CompilerParams(
            collective_id=0, has_side_effects=True, vmem_limit_bytes=60 * 2**20
        ),
        name="exchange",
    )(
        eigvecs.reshape(blocks, *block), occupations.reshape(1, depth), energies.reshape(1, depth), neighbours
    )
    per = 4
    out = jax.ShapeDtypeStruct((blocks, slots, keep, tile), F32)
    density, energy = pl.pallas_call(
        place_kernel,
        out_shape=(out, out),
        grid=(blocks // per,),
        in_specs=[pl.BlockSpec(memory_space=pltpu.SMEM), pl.BlockSpec(memory_space=pltpu.VMEM)],
        out_specs=[pl.BlockSpec((per, slots, keep, tile), lambda i: (i, 0, 0, 0))] * 2,
        name="place",
    )(pos, pltpu.with_memory_space_constraint(tiles, pltpu.VMEM))
    return density, energy


def solution(mesh):
    return jax.shard_map(
        body,
        mesh=mesh,
        in_specs=(P("atoms", "bands"), P("bands"), P("bands"), P("atoms", None)),
        out_specs=(P("atoms", None, "bands", None), P("atoms", None, "bands", None)),
        check_vma=False,
    )
```

time: 70 us -> 68.2 us (0.974)
  Pallas kernels: 68.9 us -> 67.4 us
    pallas_call x2, Pallas kernels: 68.9 us -> 67.4 us  [the longest x1 66 us: body(): pl.pallas_call(exchange_kernel, out_shape=(pltpu.VMEM((2, blocks + FAR, g...]
where the time goes in v2:
time: 68.2 us; the launch traced here: 68.1 us
  Pallas kernels  67.4 us (99%)
    pallas_call x1, Pallas kernels, body(): pl.pallas_call(exchange_kernel, out_shape=(pltpu.VMEM((2, blocks + FAR, g...  66 us
    pallas_call x1, Pallas kernels, body(): pl.pallas_call(place_kernel, out_shape=(out, out), grid=(blocks // per,),...  1.44 us

profile of v2, /device:TPU:8, one launch (start us, length us, event | category | flops | bytes accessed | tf_op | source)
XLA Modules:
  0.0 68.1 jit_solution(16749267130263162428)
XLA Ops:
  0.6 66.0 %exchange.1 = (f32[2,16,128,128]{3,2,1,0:T(8,128)S(1)}, s32[8,16]{1,0:T(8,128)S(4)}) custom-call(bf16[8,4,2,16,1024]{4,3,2,1,0:T(8,128)(2,1)} %bitcast.3, f32[1,1024]{1,0:T(1,128)} %bitcast.4, f32[1,1024]{1,0:T(1,128)} %bitcast.5, s32[8,16]{1,0:T(8,128)} %neigh.1), custom_call_target="tpu_custom_call" | custom-call | tf_op jit(solution)/shard_map/exchange/pallas_call | solution.py:339
  66.6 1.4 %place.1 = (f32[8,16,16,128]{3,2,1,0:T(8,128)}, f32[8,16,16,128]{3,2,1,0:T(8,128)}) custom-call(s32[8,16]{1,0:T(8,128)S(4)} %get-tuple-element.4.pos, f32[2,16,128,128]{3,2,1,0:T(8,128)S(1)} %get-tuple-element.5.tiles), custom_call_target="tpu_custom_call" | custom-call | tf_op jit(solution)/shard_map/place/pallas_call | solution.py:376

commit v3 on v2

--- a/solution.py
+++ b/solution.py
@@ -280,23 +280,23 @@
     forward(1)
     stages[4].relay()
     run_far(5)
+    pass_on(1)
     finish(0)
     finish(1)
     finish(2)
-    pass_on(1)
+    forward_half(0, 0)
+    stages[5].relay()
     finish(3)
-    stages[5].relay()
-    forward_half(0, 0)
     finish(4)
+    forward_half(0, 1)
     run_far(6)
-    forward_half(0, 1)
+    finish(5)
+    forward_half(1, 0)
     run_far(7)
-    finish(5)
     stages[6].relay()
-    forward_half(1, 0)
+    forward_half(1, 1)
     run_far(8)
     stages[7].relay()
-    forward_half(1, 1)
     run_far(9)
     finish_halves(0)
     stages[8].relay()

time: 68.2 us -> 65.9 us (0.966)
  Pallas kernels: 67.4 us -> 65.2 us
    pallas_call x1, Pallas kernels: 66 us -> 63.7 us  [body(): pl.pallas_call(exchange_kernel, out_shape=(pltpu.VMEM((2, blocks + FAR, g...]
where the time goes in v3:
time: 65.9 us; the launch traced here: 65.8 us
  Pallas kernels  65.2 us (99%)
    pallas_call x1, Pallas kernels, body(): pl.pallas_call(exchange_kernel, out_shape=(pltpu.VMEM((2, blocks + FAR, g...  63.7 us
    pallas_call x1, Pallas kernels, body(): pl.pallas_call(place_kernel, out_shape=(out, out), grid=(blocks // per,),...  1.44 us

profile of v3, /device:TPU:8, one launch (start us, length us, event | category | flops | bytes accessed | tf_op | source)
XLA Modules:
  0.0 65.8 jit_solution(17391054967303494741)
XLA Ops:
  0.6 63.7 %exchange.1 = (f32[2,16,128,128]{3,2,1,0:T(8,128)S(1)}, s32[8,16]{1,0:T(8,128)S(4)}) custom-call(bf16[8,4,2,16,1024]{4,3,2,1,0:T(8,128)(2,1)} %bitcast.3, f32[1,1024]{1,0:T(1,128)} %bitcast.4, f32[1,1024]{1,0:T(1,128)} %bitcast.5, s32[8,16]{1,0:T(8,128)} %neigh.1), custom_call_target="tpu_custom_call" | custom-call | tf_op jit(solution)/shard_map/exchange/pallas_call | solution.py:339
  64.4 1.4 %place.1 = (f32[8,16,16,128]{3,2,1,0:T(8,128)}, f32[8,16,16,128]{3,2,1,0:T(8,128)}) custom-call(s32[8,16]{1,0:T(8,128)S(4)} %get-tuple-element.4.pos, f32[2,16,128,128]{3,2,1,0:T(8,128)S(1)} %get-tuple-element.5.tiles), custom_call_target="tpu_custom_call" | custom-call | tf_op jit(solution)/shard_map/place/pallas_call | solution.py:376

commit v4 on v3

--- a/solution.py
+++ b/solution.py
@@ -129,8 +129,8 @@
     scale(0, own)
 
     hops = {}
-    for rank in range(2):
-        for kind in range(2):
+    for kind in range(2):
+        for rank in range(2):
             for side in range(2):
                 q = 2 * kind + side
                 if rank == 0:
@@ -195,7 +195,8 @@
             self.rows(2, 4)
             self.hop(3, self.piece(1, 1), 0)
             self.hop(2, self.piece(3, 0), 1)
-            self.rows(6, 2)
+            if self.s < WHOLE:
+                self.rows(6, 2)
 
         def relay(self):
             for which in range(2):
@@ -274,16 +275,16 @@
     stages[0].relay()
     stages[1].relay()
     run_far(4)
+    forward(1)
     stages[2].relay()
+    stages[3].relay()
+    run_far(5)
     pass_on(0)
-    stages[3].relay()
-    forward(1)
-    stages[4].relay()
-    run_far(5)
-    pass_on(1)
     finish(0)
     finish(1)
+    stages[4].relay()
     finish(2)
+    pass_on(1)
     forward_half(0, 0)
     stages[5].relay()
     finish(3)
@@ -298,8 +299,10 @@
     run_far(8)
     stages[7].relay()
     run_far(9)
+    for s in range(WHOLE, WHOLE + HALVES):
+        stages[s].rows(6, 2)
+    stages[8].relay()
     finish_halves(0)
-    stages[8].relay()
     stages[9].relay()
     finish_halves(1)
 

time: 65.9 us -> 64.6 us (0.980)
  Pallas kernels: 65.2 us -> 63.7 us
    pallas_call x1, Pallas kernels: 63.7 us -> 62.2 us  [body(): pl.pallas_call(exchange_kernel, out_shape=(pltpu.VMEM((2, blocks + FAR, g...]
where the time goes in v4:
time: 64.6 us; the launch traced here: 64.3 us
  Pallas kernels  63.7 us (99%)
    pallas_call x1, Pallas kernels, body(): pl.pallas_call(exchange_kernel, out_shape=(pltpu.VMEM((2, blocks + FAR, g...  62.2 us
    pallas_call x1, Pallas kernels, body(): pl.pallas_call(place_kernel, out_shape=(out, out), grid=(blocks // per,),...  1.44 us

profile of v4, /device:TPU:8, one launch (start us, length us, event | category | flops | bytes accessed | tf_op | source)
XLA Modules:
  0.0 64.3 jit_solution(14764894476992796082)
XLA Ops:
  0.6 62.2 %exchange.1 = (f32[2,16,128,128]{3,2,1,0:T(8,128)S(1)}, s32[8,16]{1,0:T(8,128)S(4)}) custom-call(bf16[8,4,2,16,1024]{4,3,2,1,0:T(8,128)(2,1)} %bitcast.3, f32[1,1024]{1,0:T(1,128)} %bitcast.4, f32[1,1024]{1,0:T(1,128)} %bitcast.5, s32[8,16]{1,0:T(8,128)} %neigh.1), custom_call_target="tpu_custom_call" | custom-call | tf_op jit(solution)/shard_map/exchange/pallas_call | solution.py:342
  62.9 1.4 %place.1 = (f32[8,16,16,128]{3,2,1,0:T(8,128)}, f32[8,16,16,128]{3,2,1,0:T(8,128)}) custom-call(s32[8,16]{1,0:T(8,128)S(4)} %get-tuple-element.4.pos, f32[2,16,128,128]{3,2,1,0:T(8,128)S(1)} %get-tuple-element.5.tiles), custom_call_target="tpu_custom_call" | custom-call | tf_op jit(solution)/shard_map/place/pallas_call | solution.py:379

commit v5 on v4

--- a/solution.py
+++ b/solution.py
@@ -129,7 +129,7 @@
     scale(0, own)
 
     hops = {}
-    for kind in range(2):
+    def leave(kind):
         for rank in range(2):
             for side in range(2):
                 q = 2 * kind + side
@@ -146,6 +146,7 @@
                 )
                 hops[kind, rank, side].start()
 
+    leave(0)
     for swap in swaps[:3]:
         swap.wait_recv()
     scale(1, mate)
@@ -268,7 +269,10 @@
             forwards[s, side].wait_recv()
         stages[s].run()
 
-    for s in range(own_stages):
+    swaps[3].wait_recv()
+    stages[0].run()
+    leave(1)
+    for s in range(1, own_stages):
         swaps[3 + s].wait_recv()
         stages[s].run()
     forward(0)
@@ -291,7 +295,6 @@
     finish(4)
     forward_half(0, 1)
     run_far(6)
-    finish(5)
     forward_half(1, 0)
     run_far(7)
     stages[6].relay()
@@ -299,11 +302,12 @@
     run_far(8)
     stages[7].relay()
     run_far(9)
+    stages[8].relay()
     for s in range(WHOLE, WHOLE + HALVES):
         stages[s].rows(6, 2)
-    stages[8].relay()
+    stages[9].relay()
+    finish(5)
     finish_halves(0)
-    stages[9].relay()
     finish_halves(1)
 
     for copy in asks + swaps + list(hops.values()) + list(forwards.values()) + list(y_hops.values()):

time: 64.6 us -> 64.5 us (level)
  no operation moved by 1% of the time
where the time goes in v5:
time: 64.5 us; the launch traced here: 64.4 us
  Pallas kernels  63.8 us (99%)
    pallas_call x1, Pallas kernels, body(): pl.pallas_call(exchange_kernel, out_shape=(pltpu.VMEM((2, blocks + FAR, g...  62.3 us
    pallas_call x1, Pallas kernels, body(): pl.pallas_call(place_kernel, out_shape=(out, out), grid=(blocks // per,),...  1.44 us

profile of v5, /device:TPU:8, one launch (start us, length us, event | category | flops | bytes accessed | tf_op | source)
XLA Modules:
  0.0 64.4 jit_solution(10756160717247207117)
XLA Ops:
  0.6 62.3 %exchange.1 = (f32[2,16,128,128]{3,2,1,0:T(8,128)S(1)}, s32[8,16]{1,0:T(8,128)S(4)}) custom-call(bf16[8,4,2,16,1024]{4,3,2,1,0:T(8,128)(2,1)} %bitcast.3, f32[1,1024]{1,0:T(1,128)} %bitcast.4, f32[1,1024]{1,0:T(1,128)} %bitcast.5, s32[8,16]{1,0:T(8,128)} %neigh.1), custom_call_target="tpu_custom_call" | custom-call | tf_op jit(solution)/shard_map/exchange/pallas_call | solution.py:346
  63.0 1.4 %place.1 = (f32[8,16,16,128]{3,2,1,0:T(8,128)}, f32[8,16,16,128]{3,2,1,0:T(8,128)}) custom-call(s32[8,16]{1,0:T(8,128)S(4)} %get-tuple-element.4.pos, f32[2,16,128,128]{3,2,1,0:T(8,128)S(1)} %get-tuple-element.5.tiles), custom_call_target="tpu_custom_call" | custom-call | tf_op jit(solution)/shard_map/place/pallas_call | solution.py:383
